TPU v7x, 128 devices: a whole 4x4x4 slice. The times are simulated.
128 devices in a mesh: dp: 16 (over x, y), expert: 8 (over z, core).
Axes of the slice: x: 4, y: 4, z: 4, core: 2. Of those that a mesh axis runs over, the one named last changes fastest.
Arguments:
- tokens: bfloat16 [2048, 6144], P('dp'), may hold values from -6 to 6
- routes: int32 [2048, 2], P('dp'), may hold values from 0 to 7, all different within a row; in each aligned block of 128 rows (0 to 127, 128 to 255, ...) at most 64 rows name the same one
- gates: float32 [2048, 2], P('dp'), may hold values from 0.1 to 1
- capacity: int32 [8], replicated, may hold values from 32 to 64, as said below
- w_gate: bfloat16 [8, 6144, 8192], P('expert', None, 'dp'), may hold values from -0.078125 to 0.078125
- w_up: bfloat16 [8, 6144, 8192], P('expert', None, 'dp'), may hold values from -0.078125 to 0.078125
- w_down: bfloat16 [8, 8192, 6144], P('expert', 'dp'), may hold values from -0.0625 to 0.0625
Outputs:
- mixed: bfloat16 [2048, 6144], P('dp', 'expert')
Inputs may be any that keep to these rules, and one draw needn't show every extreme that they name: `routes`: each token names two different experts. Within the 128 tokens of one index of dp no expert is named by more than 64 tokens, and in some shards one expert is named by exactly 64. Some expert's capacity is exactly 64.
All inputs are finite; a program needn't handle non-finite values.
Results may differ from a plain program's by a relative error of at most 0.015.
Values may be sent and summed in bfloat16 or wider, within the bound.
No kernel may reach another device: no remote copies, remote signals or barrier semaphores. Data moves between devices by JAX's collectives and lax.ppermute only.
A program may use at most 128 MiB of HBM per device.

v0:
```python
import jax
import jax.numpy as jnp
from jax import lax
from jax.sharding import PartitionSpec as P


def on_device(tokens, routes, gates, capacity, w_gate, w_up, w_down):
    owner_index = lax.axis_index("expert")
    group_size = lax.axis_size("expert")
    local_rows = tokens.shape[0]
    num_experts = group_size * w_gate.shape[0]
    slot_count = 4 * local_rows // num_experts
    matched = routes == owner_index
    member = jnp.any(matched, axis=-1).astype(jnp.int32)
    weight = jnp.sum(jnp.where(matched, gates, 0.0), axis=-1)
    position = jnp.cumsum(member) - member
    limit_value = jnp.sum(
        jnp.where(jnp.arange(num_experts, dtype=jnp.int32) == owner_index, capacity, 0)
    )
    retained = (member == 1) & (position < limit_value)
    slot_ids = jnp.arange(slot_count, dtype=jnp.int32)
    selector = (retained[None, :] & (position[None, :] == slot_ids[:, None])).astype(jnp.bfloat16)
    slot_rows = jnp.dot(selector, tokens, preferred_element_type=jnp.float32).astype(jnp.bfloat16)
    gate_panel = w_gate[0]
    up_panel = w_up[0]
    down_panel = w_down[0]
    block_rows = lax.all_gather(slot_rows, "dp", axis=0, tiled=True)
    gate_value = jnp.dot(block_rows, gate_panel, preferred_element_type=jnp.float32)
    up_value = jnp.dot(block_rows, up_panel, preferred_element_type=jnp.float32)
    hidden = (jax.nn.silu(gate_value) * up_value).astype(jnp.bfloat16)
    partial_value = jnp.dot(hidden, down_panel, preferred_element_type=jnp.float32)
    returned = lax.psum_scatter(
        partial_value.astype(jnp.bfloat16), "dp", scatter_dimension=0, tiled=True
    ).astype(jnp.float32)
    placed = jnp.einsum(
        "ct,cd->td", selector.astype(jnp.float32), returned, precision=lax.Precision.HIGHEST
    )
    weighted = weight[:, None] * placed
    summed = lax.psum(weighted.astype(jnp.bfloat16), "expert").astype(jnp.float32)
    feature_width = summed.shape[1] // group_size
    result = lax.dynamic_slice_in_dim(summed, owner_index * feature_width, feature_width, 1)
    return result.astype(jnp.bfloat16)


def solution(mesh):
    in_specs = (
        P("dp", None),
        P("dp", None),
        P("dp", None),
        P(),
        P("expert", None, "dp"),
        P("expert", None, "dp"),
        P("expert", "dp", None),
    )
    out_specs = P("dp", "expert")
    return jax.shard_map(
        on_device, mesh=mesh, in_specs=in_specs, out_specs=out_specs, check_vma=False
    )
```

profile of v0, /device:TPU:0, one launch (start us, length us, event | category | flops | bytes accessed | tf_op | source)
XLA Modules:
  0.0 303.3 jit_solution(16822140769576966833)
XLA Ops:
  6.5 0.0 copy-start
  6.5 0.0 all-gather.2.cloned.1.call-start
  6.5 0.8 fusion.16
  7.4 0.1 copy.9
  7.5 0.2 reduce-window.7
  7.7 0.1 reduce
  7.8 1.3 fusion.15
  9.1 0.7 compare_and_fusion
  9.7 0.0 copy-done
  9.7 1.3 convolution_convert_fusion.1
  11.0 0.0 all-gather.2.cloned.1.call-update
  11.0 0.0 reduce-scatter.2.cloned.1.call-start
  11.1 92.2 %all-gather.2.cloned.1.call-done = bf16[1024,6144]{1,0:T(8,128)(2,1)} async-done(((bf16[64,6144]{1,0:T(8,128)(2,1)}), bf16[1024,6144]{1,0:T(8,128)(2,1)}) %all-gather.2.cloned.1.call-update) | async-done | bytes 12582928 | tf_op jit(solution)/shard_map/all_gather | solution.py:27
  103.3 0.0 copy-start.3
  103.3 11.6 %fusion.2 = f32[1024,512]{1,0:T(8,128)S(1)} fusion(bf16[1024,6144]{1,0:T(8,128)(2,1)} %all-gather.2.cloned.1.call-done, bf16[1,6144,512]{2,1,0:T(8,128)(2,1)} %param.12), kind=kOutput, calls=%fused_computation.5 | convolution fusion | flops 6442450944 | bytes 20971520 | tf_op jit(solution)/shard_map/dot_general | solution.py:29
  114.9 0.0 copy-done.3
  114.9 0.0 copy-start.4
  114.9 9.0 %multiply_convert_fusion = bf16[1024,512]{1,0:T(8,128)(2,1)S(1)} fusion(f32[1024,512]{1,0:T(8,128)S(1)} %fusion.2, bf16[1024,6144]{1,0:T(8,128)(2,1)S(1)} %copy-done.3, bf16[1,6144,512]{2,1,0:T(8,128)(2,1)} %param.11), kind=kOutput, calls=%fused_computation.9 | convolution fusion | flops 6445596672 | bytes 22020096 | tf_op jit(solution)/shard_map/dot_general | solution.py:28
  124.0 0.0 copy-done.4
  124.0 9.6 %convolution_convert_fusion = bf16[1024,6144]{1,0:T(8,128)(2,1)} fusion(bf16[1024,512]{1,0:T(8,128)(2,1)S(1)} %multiply_convert_fusion, bf16[1,512,6144]{2,1,0:T(8,128)(2,1)S(1)} %copy-done.4), kind=kOutput, calls=%fused_computation | convolution fusion | flops 6448742400 | bytes 19922944 | tf_op jit(solution)/shard_map/dot_general | solution.py:31
  133.6 0.0 copy-start.1
  133.6 0.0 copy-start.2
  133.6 0.0 reduce-scatter.2.cloned.1.call-update
  133.6 0.0 all-reduce.2.cloned.1.call-start
  133.6 0.6 copy-done.1
  134.2 0.0 copy-done.2
  134.3 94.4 %reduce-scatter.2.cloned.1.call-done = bf16[64,6144]{1,0:T(8,128)(2,1)} async-done(((bf16[1024,6144]{1,0:T(8,128)(2,1)}), bf16[64,6144]{1,0:T(8,128)(2,1)}) %reduce-scatter.2.cloned.1.call-update) | async-done | bytes 786448 | tf_op jit(solution)/shard_map/reduce_scatter | solution.py:32
  228.7 2.9 fusion
  231.6 0.0 all-reduce.2.cloned.1.call-update
  231.6 63.5 %all-reduce.2.cloned.1.call-done = bf16[128,6144]{1,0:T(8,128)(2,1)} async-done(((bf16[128,6144]{1,0:T(8,128)(2,1)}), bf16[128,6144]{1,0:T(8,128)(2,1)}) %all-reduce.2.cloned.1.call-update) | async-done | bytes 1572880 | tf_op jit(solution)/shard_map/psum | solution.py:39
  295.1 1.6 convert_convert_fusion
  (3 shorter events, 0.0 us)
Async XLA Ops:
  6.5 3.2 %copy-start = (bf16[128,6144]{1,0:T(8,128)(2,1)S(1)}, bf16[128,6144]{1,0:T(8,128)(2,1)}, u32[]{:S(2)}) copy-start(bf16[128,6144]{1,0:T(8,128)(2,1)} %param.7) | copy-start | bytes 4718596
  6.5 96.8 %all-gather.2.cloned.1.call-start = ((), (), s32[]{:S(2)}) async-start(), calls=%async_computation.1 | async-start | bytes 13369344 | tf_op jit(solution)/shard_map/all_gather | solution.py:27
  11.0 217.6 %reduce-scatter.2.cloned.1.call-start = ((), (), s32[]{:S(2)}) async-start(), calls=%async_computation.2 | async-start | bytes 13369344 | tf_op jit(solution)/shard_map/reduce_scatter | solution.py:32
  103.3 11.6 %copy-start.3 = (bf16[1024,6144]{1,0:T(8,128)(2,1)S(1)}, bf16[1024,6144]{1,0:T(8,128)(2,1)}, u32[]{:S(2)}) copy-start(bf16[1024,6144]{1,0:T(8,128)(2,1)} %all-gather.2.cloned.1.call-done) | copy-start | bytes 37748740
  114.9 9.1 %copy-start.4 = (bf16[1,512,6144]{2,1,0:T(8,128)(2,1)S(1)}, bf16[1,512,6144]{2,1,0:T(8,128)(2,1)}, u32[]{:S(2)}) copy-start(bf16[1,512,6144]{2,1,0:T(8,128)(2,1)} %param.13) | copy-start | bytes 18874372
  133.6 0.7 copy-start.1
  133.6 0.7 copy-start.2
  133.6 161.5 %all-reduce.2.cloned.1.call-start = ((), (), s32[]{:S(2)}) async-start(), calls=%async_computation.3 | async-start | bytes 3145728 | tf_op jit(solution)/shard_map/psum | solution.py:39
Sparse Core Ops, SparseCore 0:
  11.2 92.1 all-gather.1
  133.7 94.9 reduce-scatter.1
  231.7 63.3 all-reduce.1
where the time goes:
time: 304 us; the launch traced here: 303 us
  waiting for transfers between devices  250 us (82%)
  matrix products  34.4 us (11%)
  between operations  13.2 us (4%)
  other arithmetic  4.69 us (2%)
    reduce_scatter x1, waiting for transfers between devices, on_device(): lax.psum_scatter(partial_value.astype(jnp.bfloat16), 'dp', scatter_dimens...  94.4 us
    all_gather x1, waiting for transfers between devices, on_device(): block_rows = lax.all_gather(slot_rows, 'dp', axis=0, tiled=True)  92.2 us
    psum x1, waiting for transfers between devices, on_device(): lax.psum(weighted.astype(jnp.bfloat16), 'expert').astype(jnp.float32)  63.5 us
    dot_general x1, matrix products, on_device(): up_value = jnp.dot(block_rows, up_panel, preferred_element_type=jnp.float32)  11.6 us
    dot_general x1, matrix products, on_device(): jnp.dot(hidden, down_panel, preferred_element_type=jnp.float32)  9.56 us
    dot_general x1, matrix products, on_device(): jnp.dot(block_rows, gate_panel, preferred_element_type=jnp.float32)  9.04 us
  transfers between devices with their start and end apart: 3, of which 3 were waited for; matrix products, arithmetic and copies ran while one was open for 0% of the time, Pallas kernels for 0%

commit v1 on v0

--- a/solution.py
+++ b/solution.py
@@ -5,6 +5,13 @@
 
 
 def on_device(tokens, routes, gates, capacity, w_gate, w_up, w_down):
+
+    def point_results_up(z_in, bus_axis):
+        sides = []
+        for _ in range(lax.axis_size(bus_axis)):
+            sides.append(z_in)
+        return jnp.concatenate(lax.all_to_all(jnp.stack(sides), bus_axis, 0, 0), axis=0)
+
     owner_index = lax.axis_index("expert")
     group_size = lax.axis_size("expert")
     local_rows = tokens.shape[0]
@@ -24,7 +31,7 @@
     gate_panel = w_gate[0]
     up_panel = w_up[0]
     down_panel = w_down[0]
-    block_rows = lax.all_gather(slot_rows, "dp", axis=0, tiled=True)
+    block_rows = point_results_up(slot_rows, "dp")
     gate_value = jnp.dot(block_rows, gate_panel, preferred_element_type=jnp.float32)
     up_value = jnp.dot(block_rows, up_panel, preferred_element_type=jnp.float32)
     hidden = (jax.nn.silu(gate_value) * up_value).astype(jnp.bfloat16)

time: 304 us -> 363 us (1.19)
  blocking collectives: 0 us -> 149 us
  waiting for transfers between devices: 250 us -> 157 us
  local copies, waits for them, and re-layouts: 0.75 us -> 6.89 us
    all_to_all x0 -> x1, blocking collectives: none -> 149 us  [point_results_up(): lax.all_to_all(jnp.stack(sides), bus_axis, 0, 0)]
    all_gather x1 -> x0, waiting for transfers between devices: 92.2 us -> none  [on_device(): block_rows = lax.all_gather(slot_rows, 'dp', axis=0, tiled=True)]
    another operation x0 -> x1, local copies, waits for them, and re-layouts: none -> 6.14 us  [point_results_up(): jnp.stack(sides)]
  transfers between devices with their start and end apart: 3 -> 2, of which waited for: 3 -> 2; matrix products, arithmetic and copies ran while one was open for 0% -> 0% of each run, Pallas kernels for 0% -> 0%
where the time goes in v1:
time: 363 us
  waiting for transfers between devices  157 us (43%)
  blocking collectives  149 us (41%)
  matrix products  31.3 us (9%)
  between operations  13.5 us (4%)
  local copies, waits for them, and re-layouts  6.89 us (2%)
  other arithmetic  4.69 us (1%)
    all_to_all x1, blocking collectives, point_results_up(): lax.all_to_all(jnp.stack(sides), bus_axis, 0, 0)  149 us
    reduce_scatter x1, waiting for transfers between devices, on_device(): lax.psum_scatter(partial_value.astype(jnp.bfloat16), 'dp', scatter_dimens...  93.9 us
    psum x1, waiting for transfers between devices, on_device(): lax.psum(weighted.astype(jnp.bfloat16), 'expert').astype(jnp.float32)  63.5 us
    dot_general x1, matrix products, on_device(): up_value = jnp.dot(block_rows, up_panel, preferred_element_type=jnp.float32)  9.96 us
    dot_general x1, matrix products, on_device(): jnp.dot(hidden, down_panel, preferred_element_type=jnp.float32)  9.65 us
    dot_general x1, matrix products, on_device(): jnp.dot(block_rows, gate_panel, preferred_element_type=jnp.float32)  8.37 us
  transfers between devices with their start and end apart: 2, of which 2 were waited for; matrix products, arithmetic and copies ran while one was open for 0% of the time, Pallas kernels for 0%

profile of v1, /device:TPU:0, one launch (start us, length us, event | category | flops | bytes accessed | tf_op | source)
XLA Modules:
  0.0 363.2 jit_solution(7021934161952952420)
XLA Ops:
  6.5 0.0 copy-start
  6.5 0.0 reduce-scatter.2.cloned.1.call-start
  6.5 0.8 fusion.16
  7.4 0.1 copy.9
  7.5 0.2 reduce-window.7
  7.7 0.1 reduce
  7.8 1.3 fusion.15
  9.1 0.7 compare_and_fusion
  9.7 0.0 copy-done
  9.7 0.4 convolution_convert_fusion.1
  10.1 6.1 %stack.2 = bf16[16,64,6144]{2,1,0:T(8,128)(2,1)} broadcast(bf16[64,6144]{1,0:T(8,128)(2,1)S(1)} %convolution_convert_fusion.1), dimensions={1,2} | broadcast | bytes 13369344 | tf_op jit(solution)/shard_map/stack | solution.py:13
  16.2 0.0 slice-start
  16.2 0.0 slice-start.2
  16.2 149.4 %all_to_all.5 = bf16[16,64,6144]{2,1,0:T(8,128)(2,1)S(1)} all-to-all(bf16[16,64,6144]{2,1,0:T(8,128)(2,1)} %stack.2), channel_id=1, replica_groups=mesh['dp'=16,'expert'=8] {'dp'}, dimensions={0} | all-to-all | bytes 25165824 | tf_op jit(solution)/shard_map/all_to_all | solution.py:13
  165.6 0.0 slice-start.1
  165.6 0.0 slice-start.3
  165.6 10.0 %fusion.2 = f32[1024,512]{1,0:T(8,128)} fusion(bf16[1024,6144]{1,0:T(8,128)(2,1)S(1)} %bitcast.19, bf16[1,6144,512]{2,1,0:T(8,128)(2,1)} %param.12), kind=kOutput, calls=%fused_computation.5 | convolution fusion | flops 6442450944 | bytes 20971520 | tf_op jit(solution)/shard_map/dot_general | solution.py:36
  175.6 0.0 slice-done
  175.6 0.0 slice-done.1
  175.6 8.4 %multiply_convert_fusion = bf16[1024,512]{1,0:T(8,128)(2,1)S(1)} fusion(f32[1024,512]{1,0:T(8,128)} %fusion.2, bf16[1024,6144]{1,0:T(8,128)(2,1)S(1)} %bitcast.20, bf16[1,6144,512]{2,1,0:T(8,128)(2,1)S(1)} %bitcast.22), kind=kOutput, calls=%fused_computation.9 | convolution fusion | flops 6445596672 | bytes 22020096 | tf_op jit(solution)/shard_map/dot_general | solution.py:35
  184.0 0.0 slice-done.2
  184.0 0.0 slice-done.3
  184.0 9.7 %convolution_convert_fusion = bf16[1024,6144]{1,0:T(8,128)(2,1)} fusion(bf16[1024,512]{1,0:T(8,128)(2,1)S(1)} %multiply_convert_fusion, bf16[1,512,6144]{2,1,0:T(8,128)(2,1)S(1)} %bitcast.24), kind=kOutput, calls=%fused_computation | convolution fusion | flops 6448742400 | bytes 19922944 | tf_op jit(solution)/shard_map/dot_general | solution.py:38
  193.7 0.0 copy-start.1
  193.7 0.0 copy-start.2
  193.7 0.0 reduce-scatter.2.cloned.1.call-update
  193.7 0.0 all-reduce.2.cloned.1.call-start
  193.7 0.6 copy-done.1
  194.3 0.0 copy-done.2
  194.4 93.9 %reduce-scatter.2.cloned.1.call-done = bf16[64,6144]{1,0:T(8,128)(2,1)} async-done(((bf16[1024,6144]{1,0:T(8,128)(2,1)}), bf16[64,6144]{1,0:T(8,128)(2,1)}) %reduce-scatter.2.cloned.1.call-update) | async-done | bytes 786448 | tf_op jit(solution)/shard_map/reduce_scatter | solution.py:39
  288.3 2.9 fusion
  291.2 0.0 all-reduce.2.cloned.1.call-update
  291.3 63.5 %all-reduce.2.cloned.1.call-done = bf16[128,6144]{1,0:T(8,128)(2,1)} async-done(((bf16[128,6144]{1,0:T(8,128)(2,1)}), bf16[128,6144]{1,0:T(8,128)(2,1)}) %all-reduce.2.cloned.1.call-update) | async-done | bytes 1572880 | tf_op jit(solution)/shard_map/psum | solution.py:46
  354.8 1.6 convert_convert_fusion
  (5 shorter events, 0.0 us)
Async XLA Ops:
  6.5 3.2 copy-start
  6.5 281.8 %reduce-scatter.2.cloned.1.call-start = ((), (), s32[]{:S(2)}) async-start(), calls=%async_computation.2 | async-start | bytes 13369344 | tf_op jit(solution)/shard_map/reduce_scatter | solution.py:39
  16.2 159.4 %slice-start = ((s8[6291456]{0:T(1024)(128)(4,1)}), s8[4194304]{0:T(1024)(128)(4,1)S(1)}, s32[]{:S(2)}) async-start(s8[6291456]{0:T(1024)(128)(4,1)} %bitcast.21), calls=%async_computation.4 | async-start | bytes 8388608
  16.2 167.7 %slice-start.2 = ((s8[6291456]{0:T(1024)(128)(4,1)}), s8[4194304]{0:T(1024)(128)(4,1)S(1)}, s32[]{:S(2)}) async-start(s8[6291456]{0:T(1024)(128)(4,1)} %bitcast.23), calls=%async_computation.6 | async-start | bytes 8388608
  165.6 10.0 %slice-start.1 = ((s8[6291456]{0:T(1024)(128)(4,1)}), s8[2097152]{0:T(1024)(128)(4,1)S(1)}, s32[]{:S(2)}) async-start(s8[6291456]{0:T(1024)(128)(4,1)} %bitcast.21), calls=%async_computation.5 | async-start | bytes 4194304
  165.6 18.4 %slice-start.3 = ((s8[6291456]{0:T(1024)(128)(4,1)}), s8[2097152]{0:T(1024)(128)(4,1)S(1)}, s32[]{:S(2)}) async-start(s8[6291456]{0:T(1024)(128)(4,1)} %bitcast.23), calls=%async_computation.7 | async-start | bytes 4194304
  193.7 0.7 copy-start.1
  193.7 0.7 copy-start.2
  193.7 161.1 %all-reduce.2.cloned.1.call-start = ((), (), s32[]{:S(2)}) async-start(), calls=%async_computation.3 | async-start | bytes 3145728 | tf_op jit(solution)/shard_map/psum | solution.py:46
Sparse Core Ops, SparseCore 0:
  193.8 94.4 reduce-scatter.1
  291.4 63.3 all-reduce.1
